TPU v7x, 32 devices: a whole 2x2x4 slice. The times are simulated.
32 devices in a mesh: groups: 2 (over x), seq: 16 (over z, y, core).
Axes of the slice: x: 2, y: 2, z: 4, core: 2. Of those that a mesh axis runs over, the one named last changes fastest.
Arguments:
- enc_input: bfloat16 [8192, 1408], P(('groups', 'seq')), parts along dimension 0, may hold values from -6 to 6
- enc_weight: bfloat16 [2816, 1536], P('seq'), may hold values from -0.109375 to 0.109375
- norm_gain: float32 [1536], replicated, may hold values from 0.5 to 1.5
- q_weight: bfloat16 [1536, 1024], replicated, may hold values from -1 to 1
- kv_weight: bfloat16 [1536, 320], replicated, may hold values from -1 to 1
- out_weight: bfloat16 [1536, 1536], replicated, may hold values from -0.15625 to 0.15625
- dec_weight: float32 [3, 1536], replicated, may hold values from -3 to 3
- track_weight: bfloat16 [192, 1536], P('seq'), may hold values from -0.15625 to 0.15625
- track_grad: bfloat16 [4096, 192], P('groups', 'seq'), parts along dimension 0, may hold values from -6 to 6
- track_index: int32 [384], P('groups'), parts along dimension 0, may hold values from 0 to 191, each once
- track_mask: int32 [384], P('groups'), parts along dimension 0, may hold values 0 or 1
Outputs:
- trunk_out: bfloat16 [4096, 1536], P(('groups', 'seq')), parts along dimension 0
- skip_grad: bfloat16 [4096, 1536], P(('groups', 'seq')), parts along dimension 0
- dec_weight_grad: float32 [6, 1536], P('groups'), parts along dimension 0
There are 2 independent parts, one for each index of `groups`. A program takes and returns all parts, laid end to end along the dimension named above; an argument that names none is the same for every part. Nothing has to cross between parts.
Inputs may be any that keep to these rules, and one draw needn't show every extreme that they name: `track_index`: names every track once.
All inputs are finite; a program needn't handle non-finite values.
Results may differ from a plain program's by a relative error of at most 0.02.
Values may be sent and summed in bfloat16 or wider, within the bound.
No kernel may reach another device: no remote copies, remote signals or barrier semaphores. Data moves between devices by JAX's collectives and lax.ppermute only.
A program may use at most 128 MiB of HBM per device.

v0:
```python
import math
import jax
import jax.numpy as jnp
from jax import lax
from jax.sharding import PartitionSpec as P

HEADS = 8
QK = 128
VDIM = 192
DILATION_SPAN = 8


def with_halo(cells, sides, width):
    for axis, dim in sides:
        count = lax.axis_size(axis)
        ends = count - 1
        head = lax.slice_in_dim(cells, 0, width, axis=dim)
        tail = lax.slice_in_dim(cells, cells.shape[dim] - width, cells.shape[dim], axis=dim)
        cells = jnp.concatenate(
            [
                lax.ppermute(tail, axis, [(i, (i + 1) % count) for i in range(ends)]),
                cells,
                lax.ppermute(head, axis, [((i + 1) % count, i) for i in range(ends)]),
            ],
            axis=dim,
        )
    return cells


def gelu_tanh(values):
    return jax.nn.gelu(values, approximate=True)


def attention(tokens, tok_f, norm_gain, q_weight, kv_weight, out_weight):
    token_rows = tokens.shape[0]
    normed = (
        tok_f * lax.rsqrt(jnp.mean(tok_f * tok_f, axis=-1, keepdims=True) + 1e-06) * norm_gain
    ).astype(jnp.bfloat16)
    query = jnp.dot(normed, q_weight, preferred_element_type=jnp.float32).astype(jnp.bfloat16)
    keyval = jnp.dot(normed, kv_weight, preferred_element_type=jnp.float32).astype(jnp.bfloat16)
    query_rows = query.reshape(token_rows * HEADS, QK)

    def block_update(carry, key_block):
        running_max, running_sum, weighted = carry
        scores = lax.dot_general(
            query_rows,
            key_block[:, :QK],
            (((1,), (1,)), ((), ())),
            preferred_element_type=jnp.float32,
        ) * QK ** (-0.5)
        new_max = jnp.maximum(running_max, jnp.max(scores, axis=1))
        shrink = jnp.exp(running_max - new_max)
        expw = jnp.exp(scores - new_max[:, None])
        running_sum = running_sum * shrink + jnp.sum(expw, axis=1)
        weighted = weighted * shrink[:, None] + jnp.dot(
            expw.astype(jnp.bfloat16), key_block[:, QK:], preferred_element_type=jnp.float32
        )
        return (new_max, running_sum, weighted)

    start_state = (
        jnp.full((token_rows * HEADS,), -1e30, jnp.float32),
        jnp.zeros((token_rows * HEADS,), jnp.float32),
        jnp.zeros((token_rows * HEADS, VDIM), jnp.float32),
    )
    carry = start_state
    piece = lax.all_gather(keyval, "seq", axis=0, tiled=True)
    count = piece.shape[0]

    def step_fn(inner, key_block):
        return (block_update(inner, key_block), 0)

    carry, unused = lax.scan(step_fn, carry, piece.reshape(count // 128, 128, piece.shape[1]))
    running_max, running_sum, weighted = carry
    context = (
        (weighted / running_sum[:, None]).reshape(token_rows, HEADS * VDIM).astype(jnp.bfloat16)
    )
    return (tok_f + jnp.dot(context, out_weight, preferred_element_type=jnp.float32)).astype(
        jnp.bfloat16
    )


def decoder_back(tok_f, dec_weight, track_weight, track_grad, track_index, track_mask):
    token_rows = tok_f.shape[0]
    exchanged = lax.all_to_all(track_grad, "seq", split_axis=0, concat_axis=1, tiled=True)
    masked = exchanged * track_mask.astype(jnp.bfloat16)[None, :]
    every_row = lax.all_gather(track_weight, "seq", axis=0, tiled=True)
    selected = jnp.take(every_row, track_index, axis=0)
    head_f = jnp.dot(masked, selected, preferred_element_type=jnp.float32)
    head_gradient = head_f.astype(jnp.bfloat16)
    padded_input = with_halo(head_gradient, (("seq", 0),), DILATION_SPAN).astype(jnp.float32)
    skip_act, pullback = jax.vjp(gelu_tanh, tok_f)
    convback = jnp.zeros(tok_f.shape, jnp.float32)
    tap_terms = []
    for shift_amount in range(3):
        shifted_rows = padded_input[
            DILATION_SPAN * (2 - shift_amount) : DILATION_SPAN * (2 - shift_amount) + token_rows
        ]
        convback = convback + dec_weight[shift_amount][None, :] * shifted_rows
        tap_terms.append(jnp.sum(skip_act * shifted_rows, axis=0))
    skip_grad = pullback(convback)[0].astype(jnp.bfloat16)
    summed = lax.psum(jnp.stack(tap_terms, axis=0), "seq")
    dec_weight_grad = summed / jnp.float32(math.sqrt(token_rows * lax.axis_size("seq")))
    return (skip_grad, dec_weight_grad)


def shards(
    enc_input,
    enc_weight,
    norm_gain,
    q_weight,
    kv_weight,
    out_weight,
    dec_weight,
    track_weight,
    track_grad,
    track_index,
    track_mask,
):
    token_rows = enc_input.shape[0] // 2
    patches = enc_input.reshape(token_rows, 2 * enc_input.shape[1])
    tok_sum = jnp.dot(
        patches,
        lax.all_gather(enc_weight, "seq", axis=0, tiled=True),
        preferred_element_type=jnp.float32,
    )
    tokens = tok_sum.astype(jnp.bfloat16)
    tok_f = tokens.astype(jnp.float32)
    trunk_out = attention(tokens, tok_f, norm_gain, q_weight, kv_weight, out_weight)
    skip_grad, dec_weight_grad = decoder_back(
        tok_f, dec_weight, track_weight, track_grad, track_index, track_mask
    )
    return (trunk_out, skip_grad, dec_weight_grad)


def solution(mesh):
    return jax.shard_map(
        shards,
        mesh=mesh,
        in_specs=(
            P(("groups", "seq"), None),
            P("seq", None),
            P(),
            P(),
            P(),
            P(),
            P(),
            P("seq", None),
            P("groups", "seq"),
            P("groups"),
            P("groups"),
        ),
        out_specs=(P(("groups", "seq"), None), P(("groups", "seq"), None), P("groups", None)),
        check_vma=False,
    )
```

profile of v0, /device:TPU:0, one launch (start us, length us, event | category | flops | bytes accessed | tf_op | source)
XLA Modules:
  0.0 272.7 jit_solution(8789962556055584525)
XLA Ops:
  7.9 1.1 copy.22
  9.6 7.4 %all-to-all-start = ((bf16[16,128,12]{1,2,0:T(8,128)(2,1)}), bf16[16,128,12]{1,2,0:T(8,128)(2,1)S(1)}, u32[]{:S(2)}, u32[]{:S(2)}) async-start(bf16[16,128,12]{1,2,0:T(8,128)(2,1)} %copy.20), calls=%async_computation | async-start | bytes 131072 | tf_op jit(solution)/shard_map/all_to_all | solution.py:84
  17.1 30.1 %all-gather = bf16[16,12,1536]{2,1,0:T(8,128)(2,1)} all-gather(bf16[1,12,1536]{2,1,0:T(8,128)(2,1)} %bitcast.28), channel_id=1, replica_groups=mesh['groups'=2,'seq'=16] {'seq'}, dimensions={0}, use_global_device_ids=true | all-gather | bytes 626688 | tf_op jit(solution)/shard_map/all_gather | solution.py:86
  47.2 2.0 reshape.51
  51.3 3.6 %gather_fusion = bf16[192,1536]{1,0:T(8,128)(2,1)} fusion(bf16[192,1536]{1,0:T(8,128)(2,1)} %reshape.51, s32[1024]{0:T(1024)S(1)} %pad_clamp_fusion), kind=kCustom, calls=%fused_computation | custom fusion | bytes 1180416 | tf_op jit(solution)/shard_map/jit(_take)/gather | solution.py:87
  55.5 1.5 convolution_convert_fusion.1
  57.7 2.8 %collective-permute-start = (bf16[8,1536]{1,0:T(8,128)(2,1)}, bf16[8,1536]{1,0:T(8,128)(2,1)}, u32[]{:S(2)}, u32[]{:S(2)}) collective-permute-start(bf16[8,1536]{1,0:T(8,128)(2,1)} %get-tuple-element.101), channel_id=1, source_target_pairs={{0,1},{1,2},{2,3},{3,4},{4,5},{5,6},{6,7},{7,8},{8,9},{9,10},{10,1... | collective-permute-start | bytes 73736 | tf_op jit(solution)/shard_map/ppermute | solution.py:21
  60.5 1.3 collective-permute-start.1
  61.7 1.5 slice_reduce_fusion.2
  63.2 2.1 reshape.38
  65.4 1.8 maximum_convert_fusion
  67.2 26.1 %all-gather.4.cloned.1.call-done = bf16[2816,1536]{1,0:T(8,128)(2,1)} async-done(((bf16[176,1536]{1,0:T(8,128)(2,1)}), bf16[2816,1536]{1,0:T(8,128)(2,1)}) %all-gather.4.cloned.1.call-update) | async-done | bytes 8650768 | tf_op jit(solution)/shard_map/all_gather | solution.py:123
  93.3 7.5 %multiply_reduce_fusion.3 = (f32[1536]{0:T(1024)S(1)}, f32[1536]{0:T(1024)S(1)}, f32[1536]{0:T(1024)S(1)}, f32[128]{0:T(128)S(1)}, bf16[128,1536]{1,0:T(8,128)(2,1)}, /*index=5*/f32[128,1536]{1,0:T(8,128)S(1)}) fusion(f32[144,1536]{1,0:T(8,128)} %maximum_convert_fusion, f32[1536]{0:T(1024)S(1)} %get-tuple-element.82, f32[1536]{0:T(1024)} %get-tuple-element.83, ...), kind=kOutput, calls=%fused_computation.34 | convolution fusion | flops 1114172800 | bytes 12947968 | tf_op jit(solution)/shard_map/dot_general | solution.py:121
  101.6 1.1 convolution_convert_fusion.3
  102.8 2.5 convolution_convert_fusion.2
  105.3 1.1 reshape.40
  106.4 59.2 %psum.7 = f32[3,1536]{1,0:T(4,128)S(1)} all-reduce(f32[3,1536]{1,0:T(4,128)S(1)} %pad_maximum_fusion), channel_id=1, replica_groups=mesh['groups'=2,'seq'=16] {'seq'}, use_global_device_ids=true, to_apply=%region_8.9 | all-reduce | flops 4608 | bytes 36864 | tf_op jit(solution)/shard_map/psum | solution.py:101
  166.2 2.6 copy.21
  168.7 89.4 %while.15 = (s32[]{:T(128)}, f32[1024]{0:T(1024)S(1)}, f32[1024]{0:T(1024)S(1)}, f32[1024,192]{0,1:T(8,128)}, bf16[16,128,320]{2,1,0:T(8,128)(2,1)}, /*index=5*/bf16[1024,128]{1,0:T(8,128)(2,1)S(1)}, s32[]{:T(128)}, s32[]{:T(128)}) while((s32[]{:T(128)}, f32[1024]{0:T(1024)S(1)}, f32[1024]{0:T(1024)S(1)}, f32[1024,192]{0,1:T(8,128)}, ...), condition=%wide.region_4.5_spmd.clone, body=%wide.region_1.4_spmd.clone.sunk | while | flops 85267456 | bytes 3735653 | solution.py:72
  169.7 1.0 fusion.40
  170.7 1.1 fusion.41
  171.9 2.2 convolution_add_fusion.3
  175.0 1.0 fusion.40
  176.1 1.1 fusion.41
  177.2 2.5 convolution_add_fusion.3
  180.6 1.0 fusion.40
  181.7 1.1 fusion.41
  182.8 2.5 convolution_add_fusion.3
  186.2 1.0 fusion.40
  187.3 1.1 fusion.41
  188.4 2.5 convolution_add_fusion.3
  191.8 1.0 fusion.40
  192.9 1.1 fusion.41
  194.0 2.5 convolution_add_fusion.3
  197.4 1.0 fusion.40
  198.5 1.1 fusion.41
  199.6 2.5 convolution_add_fusion.3
  203.0 1.0 fusion.40
  204.1 1.1 fusion.41
  205.2 2.5 convolution_add_fusion.3
  208.6 1.0 fusion.40
  209.7 1.1 fusion.41
  210.8 2.5 convolution_add_fusion.3
  214.2 1.0 fusion.40
  215.3 1.1 fusion.41
  216.4 2.5 convolution_add_fusion.3
  219.8 1.0 fusion.40
  220.9 1.1 fusion.41
  222.0 2.5 convolution_add_fusion.3
  226.5 1.1 fusion.41
  227.6 2.5 convolution_add_fusion.3
  232.1 1.1 fusion.41
  233.2 2.5 convolution_add_fusion.3
  237.7 1.1 fusion.41
  238.8 2.5 convolution_add_fusion.3
  243.3 1.1 fusion.41
  244.4 2.5 convolution_add_fusion.3
  248.9 1.1 fusion.41
  250.0 2.5 convolution_add_fusion.3
  254.5 1.1 fusion.41
  255.6 2.5 convolution_add_fusion.3
  258.1 1.2 divide_convert_fusion
  260.3 1.5 convert_element_type.46
  261.8 4.1 %fusion.8 = bf16[128,1536]{1,0:T(8,128)(2,1)} fusion(f32[128,1536]{1,0:T(8,128)} %copy-done.1, bf16[128,1536]{1,0:T(8,128)(2,1)S(1)} %convert_element_type.46, bf16[1536,1536]{1,0:T(8,128)(2,1)} %param.18), kind=kOutput, calls=%fused_computation.19 | convolution fusion | flops 604372992 | bytes 6291456 | tf_op jit(solution)/shard_map/dot_general | solution.py:77
  (104 shorter events, 28.3 us)
Async XLA Ops:
  7.2 95.6 %copy-start = (bf16[1536,1024]{1,0:T(8,128)(2,1)S(1)}, bf16[1536,1024]{1,0:T(8,128)(2,1)}, u32[]{:S(2)}) copy-start(bf16[1536,1024]{1,0:T(8,128)(2,1)} %param.16) | copy-start | bytes 9437188
  7.2 86.1 %all-gather.4.cloned.1.call-start = ((), (), s32[]{:S(2)}) async-start(), calls=%async_computation.1 | async-start | bytes 9191424 | tf_op jit(solution)/shard_map/all_gather | solution.py:123
  9.6 45.3 %all-to-all-start = ((bf16[16,128,12]{1,2,0:T(8,128)(2,1)}), bf16[16,128,12]{1,2,0:T(8,128)(2,1)S(1)}, u32[]{:S(2)}, u32[]{:S(2)}) async-start(bf16[16,128,12]{1,2,0:T(8,128)(2,1)} %copy.20), calls=%async_computation | async-start | bytes 131072 | tf_op jit(solution)/shard_map/all_to_all | solution.py:84
  17.0 149.2 %all-gather.6.cloned.1.call-start = ((), (), s32[]{:S(2)}) async-start(), calls=%async_computation.2 | async-start | bytes 1392640 | tf_op jit(solution)/shard_map/all_gather | solution.py:66
  57.7 7.7 %collective-permute-start = (bf16[8,1536]{1,0:T(8,128)(2,1)}, bf16[8,1536]{1,0:T(8,128)(2,1)}, u32[]{:S(2)}, u32[]{:S(2)}) collective-permute-start(bf16[8,1536]{1,0:T(8,128)(2,1)} %get-tuple-element.101), channel_id=1, source_target_pairs={{0,1},{1,2},{2,3},{3,4},{4,5},{5,6},{6,7},{7,8},{8,9},{9,10},{10,1... | collective-permute-start | bytes 73736 | tf_op jit(solution)/shard_map/ppermute | solution.py:21
  60.5 4.9 %collective-permute-start.1 = (bf16[8,1536]{1,0:T(8,128)(2,1)}, bf16[8,1536]{1,0:T(8,128)(2,1)}, u32[]{:S(2)}, u32[]{:S(2)}) collective-permute-start(bf16[8,1536]{1,0:T(8,128)(2,1)} %get-tuple-element.102), channel_id=1, source_target_pairs={{1,0},{2,1},{3,2},{4,3},{5,4},{6,5},{7,6},{8,7},{9,8},{10,9},{11,1... | collective-permute-start | bytes 73736 | tf_op jit(solution)/shard_map/ppermute | solution.py:23
  93.3 8.3 %copy-start.2 = (bf16[1536,320]{0,1:T(8,128)(2,1)S(1)}, bf16[1536,320]{0,1:T(8,128)(2,1)}, u32[]{:S(2)}) copy-start(bf16[1536,320]{0,1:T(8,128)(2,1)} %param.17) | copy-start | bytes 2949124
  93.3 8.3 %copy-start.3 = (f32[1536]{0:T(1024)S(1)}, f32[1536]{0:T(1024)}, u32[]{:S(2)}) copy-start(f32[1536]{0:T(1024)} %param.15) | copy-start | bytes 18436
  100.7 0.9 copy-start.1
Sparse Core Ops, SparseCore 0:
  10.3 82.9 all-gather.3
  102.9 36.2 all-gather.5
where the time goes:
time: 275 us; the launch traced here: 273 us
  blocking collectives  89.3 us (32%)
  matrix products  72.9 us (27%)
  local copies, waits for them, and re-layouts  33.7 us (12%)
  waiting for transfers between devices  26.8 us (10%)
  other arithmetic  24.2 us (9%)
  between operations  14.2 us (5%)
  starting transfers between devices  11.6 us (4%)
    psum x1, blocking collectives, decoder_back(): summed = lax.psum(jnp.stack(tap_terms, axis=0), 'seq')  59.2 us
    dot_general x16, matrix products, block_update(): jnp.dot(expw.astype(jnp.bfloat16), key_block[:, QK:], preferred_element_t...  39.6 us
    all_gather x1, blocking collectives, decoder_back(): every_row = lax.all_gather(track_weight, 'seq', axis=0, tiled=True)  30.1 us
    all_gather x1, waiting for transfers between devices, shards(): lax.all_gather(enc_weight, 'seq', axis=0, tiled=True)  26.1 us
    reduce_sum x16, other arithmetic, block_update(): running_sum = running_sum * shrink + jnp.sum(expw, axis=1)  18.2 us
    dot_general x16, matrix products, block_update(): lax.dot_general(query_rows, key_block[:, :QK], (((1,), (1,)), ((), ())),...  16.7 us
    squeeze x16, local copies, waits for them, and re-layouts, attention(): lax.scan(step_fn, carry, piece.reshape(count // 128, 128, piece.shape[1]))  14.4 us
    dot_general x1, matrix products, shards(): jnp.dot(patches, lax.all_gather(enc_weight, 'seq', axis=0, tiled=True), p...  7.46 us
  transfers between devices with their start and end apart: 5, of which 1 were waited for; matrix products, arithmetic and copies ran while one was open for 8% of the time, Pallas kernels for 0%

commit v1 on v0

--- a/solution.py
+++ b/solution.py
@@ -83,7 +83,22 @@
     token_rows = tok_f.shape[0]
     exchanged = lax.all_to_all(track_grad, "seq", split_axis=0, concat_axis=1, tiled=True)
     masked = exchanged * track_mask.astype(jnp.bfloat16)[None, :]
-    every_row = lax.all_gather(track_weight, "seq", axis=0, tiled=True)
+    ways, here, step = (lax.axis_size("seq"), lax.axis_index("seq"), track_weight.shape[0])
+    shape = [n * ways if d == 0 else n for d, n in enumerate(track_weight.shape)]
+    every_row = lax.dynamic_update_slice_in_dim(
+        jnp.zeros(shape, track_weight.dtype), track_weight, here * step, axis=0
+    )
+    going_up = going_down = track_weight
+    for far in range(1, ways // 2 + 1):
+        going_up = lax.ppermute(going_up, "seq", [(d, (d + 1) % ways) for d in range(ways)])
+        every_row = lax.dynamic_update_slice_in_dim(
+            every_row, going_up, (here - far) % ways * step, axis=0
+        )
+        if 2 * far < ways:
+            going_down = lax.ppermute(going_down, "seq", [(d, (d - 1) % ways) for d in range(ways)])
+            every_row = lax.dynamic_update_slice_in_dim(
+                every_row, going_down, (here + far) % ways * step, axis=0
+            )
     selected = jnp.take(every_row, track_index, axis=0)
     head_f = jnp.dot(masked, selected, preferred_element_type=jnp.float32)
     head_gradient = head_f.astype(jnp.bfloat16)

time: 275 us -> 291 us (1.058)
  starting transfers between devices: 11.6 us -> 41.5 us
  blocking collectives: 89.3 us -> 64.1 us
  local copies, waits for them, and re-layouts: 33.7 us -> 57.3 us
  waiting for transfers between devices: 26.8 us -> 11.8 us
    ppermute x0 -> x15, starting transfers between devices: none -> 32.5 us  [the longest x7 32 us: decoder_back(): lax.ppermute(going_down, 'seq', [(d, (d - 1) % ways) for d in range(ways)])]
    all_gather x1 -> x0, blocking collectives: 30.1 us -> none  [decoder_back(): every_row = lax.all_gather(track_weight, 'seq', axis=0, tiled=True)]
    all_gather x1, waiting for transfers between devices: 26.1 us -> 0.01 us  [shards(): lax.all_gather(enc_weight, 'seq', axis=0, tiled=True)]
    dynamic_update_slice x0 -> x16, local copies, waits for them, and re-layouts: none -> 24.1 us  [the longest x8 12 us: decoder_back(): lax.dynamic_update_slice_in_dim(every_row, going_up, (here - far) % ways...]
    ppermute x0 -> x15, waiting for transfers between devices: none -> 11 us  [the longest x8 8.22 us: decoder_back(): lax.ppermute(going_up, 'seq', [(d, (d + 1) % ways) for d in range(ways)])]
    psum x1, blocking collectives: 59.2 us -> 64.1 us  [decoder_back(): summed = lax.psum(jnp.stack(tap_terms, axis=0), 'seq')]
    unnamed x11 -> x18, local copies, waits for them, and re-layouts: 6.52 us -> 4.94 us
  transfers between devices with their start and end apart: 5 -> 20, of which waited for: 1 -> 7; matrix products, arithmetic and copies ran while one was open for 8% -> 16% of each run, Pallas kernels for 0% -> 0%
where the time goes in v1:
time: 291 us; the launch traced here: 287 us
  matrix products  72.4 us (25%)
  blocking collectives  64.1 us (22%)
  local copies, waits for them, and re-layouts  57.3 us (20%)
  starting transfers between devices  41.5 us (14%)
  other arithmetic  25.9 us (9%)
  between operations  14.2 us (5%)
  waiting for transfers between devices  11.8 us (4%)
    psum x1, blocking collectives, decoder_back(): summed = lax.psum(jnp.stack(tap_terms, axis=0), 'seq')  64.1 us
    dot_general x16, matrix products, block_update(): jnp.dot(expw.astype(jnp.bfloat16), key_block[:, QK:], preferred_element_t...  39.4 us
    ppermute x7, starting transfers between devices, decoder_back(): lax.ppermute(going_down, 'seq', [(d, (d - 1) % ways) for d in range(ways)])  32 us
    reduce_sum x16, other arithmetic, block_update(): running_sum = running_sum * shrink + jnp.sum(expw, axis=1)  18.2 us
    dot_general x16, matrix products, block_update(): lax.dot_general(query_rows, key_block[:, :QK], (((1,), (1,)), ((), ())),...  16.3 us
    squeeze x16, local copies, waits for them, and re-layouts, attention(): lax.scan(step_fn, carry, piece.reshape(count // 128, 128, piece.shape[1]))  14.4 us
    dynamic_update_slice x8, local copies, waits for them, and re-layouts, decoder_back(): lax.dynamic_update_slice_in_dim(every_row, going_up, (here - far) % ways...  12 us
    dynamic_update_slice x7, local copies, waits for them, and re-layouts, decoder_back(): lax.dynamic_update_slice_in_dim(every_row, going_down, (here + far) % way...  10.6 us
  transfers between devices with their start and end apart: 20, of which 7 were waited for; matrix products, arithmetic and copies ran while one was open for 16% of the time, Pallas kernels for 0%

profile of v1, /device:TPU:0, one launch (start us, length us, event | category | flops | bytes accessed | tf_op | source)
XLA Modules:
  0.0 287.3 jit_solution(6974486364475899879)
XLA Ops:
  8.4 5.1 %collective-permute-start.1 = (bf16[12,1536]{1,0:T(8,128)(2,1)}, bf16[12,1536]{1,0:T(8,128)(2,1)S(1)}, u32[]{:S(2)}, u32[]{:S(2)}) collective-permute-start(bf16[12,1536]{1,0:T(8,128)(2,1)} %param.20), channel_id=1, source_target_pairs={{0,15},{1,0},{2,1},{3,2},{4,3},{5,4},{6,5},{7,6},{8,7},{9,8},{10,9... | collective-permute-start | bytes 110600 | tf_op jit(solution)/shard_map/ppermute | solution.py:98
  13.5 2.0 collective-permute-done
  15.5 4.4 %collective-permute-start.3 = (bf16[12,1536]{1,0:T(8,128)(2,1)S(1)}, bf16[12,1536]{1,0:T(8,128)(2,1)S(1)}, u32[]{:S(2)}, u32[]{:S(2)}) collective-permute-start(bf16[12,1536]{1,0:T(8,128)(2,1)S(1)} %collective-permute-done.1), channel_id=1, source_target_pairs={{0,15},{1,0},{2,1},{3,2},{4,3},{5,4},{6,5},{7,6},{8,7},{9,8},{10,9... | collective-permute-start | bytes 110600 | tf_op jit(solution)/shard_map/ppermute | solution.py:98
  19.9 1.8 collective-permute-done.2
  21.7 4.4 %collective-permute-start.5 = (bf16[12,1536]{1,0:T(8,128)(2,1)S(1)}, bf16[12,1536]{1,0:T(8,128)(2,1)S(1)}, u32[]{:S(2)}, u32[]{:S(2)}) collective-permute-start(bf16[12,1536]{1,0:T(8,128)(2,1)S(1)} %collective-permute-done.3), channel_id=1, source_target_pairs={{0,15},{1,0},{2,1},{3,2},{4,3},{5,4},{6,5},{7,6},{8,7},{9,8},{10,9... | collective-permute-start | bytes 110600 | tf_op jit(solution)/shard_map/ppermute | solution.py:98
  26.1 2.6 collective-permute-done.4
  29.6 4.5 %collective-permute-start.7 = (bf16[12,1536]{1,0:T(8,128)(2,1)S(1)}, bf16[12,1536]{1,0:T(8,128)(2,1)}, u32[]{:S(2)}, u32[]{:S(2)}) collective-permute-start(bf16[12,1536]{1,0:T(8,128)(2,1)S(1)} %collective-permute-done.5), channel_id=1, source_target_pairs={{0,15},{1,0},{2,1},{3,2},{4,3},{5,4},{6,5},{7,6},{8,7},{9,8},{10,9... | collective-permute-start | bytes 110600 | tf_op jit(solution)/shard_map/ppermute | solution.py:98
  34.1 1.9 collective-permute-done.6
  36.6 5.8 %all-to-all-start = ((bf16[16,128,12]{1,2,0:T(8,128)(2,1)}), bf16[16,128,12]{1,2,0:T(8,128)(2,1)S(1)}, u32[]{:S(2)}, u32[]{:S(2)}) async-start(bf16[16,128,12]{1,2,0:T(8,128)(2,1)} %copy.17), calls=%async_computation | async-start | bytes 131072 | tf_op jit(solution)/shard_map/all_to_all | solution.py:84
  42.5 4.4 %collective-permute-start.9 = (bf16[12,1536]{1,0:T(8,128)(2,1)}, bf16[12,1536]{1,0:T(8,128)(2,1)S(1)}, u32[]{:S(2)}, u32[]{:S(2)}) collective-permute-start(bf16[12,1536]{1,0:T(8,128)(2,1)} %collective-permute-done.7), channel_id=1, source_target_pairs={{0,15},{1,0},{2,1},{3,2},{4,3},{5,4},{6,5},{7,6},{8,7},{9,8},{10,9... | collective-permute-start | bytes 110600 | tf_op jit(solution)/shard_map/ppermute | solution.py:98
  47.6 1.4 collective-permute-done.9
  49.6 4.4 %collective-permute-start.11 = (bf16[12,1536]{1,0:T(8,128)(2,1)S(1)}, bf16[12,1536]{1,0:T(8,128)(2,1)}, u32[]{:S(2)}, u32[]{:S(2)}) collective-permute-start(bf16[12,1536]{1,0:T(8,128)(2,1)S(1)} %collective-permute-done.9), channel_id=1, source_target_pairs={{0,15},{1,0},{2,1},{3,2},{4,3},{5,4},{6,5},{7,6},{8,7},{9,8},{10,9... | collective-permute-start | bytes 110600 | tf_op jit(solution)/shard_map/ppermute | solution.py:98
  54.1 1.3 compare_and_fusion
  55.4 1.4 collective-permute-done.11
  56.7 4.7 %collective-permute-start.13 = (bf16[12,1536]{1,0:T(8,128)(2,1)}, bf16[12,1536]{1,0:T(8,128)(2,1)}, u32[]{:S(2)}, u32[]{:S(2)}) collective-permute-start(bf16[12,1536]{1,0:T(8,128)(2,1)} %collective-permute-done.11), channel_id=1, source_target_pairs={{0,15},{1,0},{2,1},{3,2},{4,3},{5,4},{6,5},{7,6},{8,7},{9,8},{10,9... | collective-permute-start | bytes 110600 | tf_op jit(solution)/shard_map/ppermute | solution.py:98
  62.1 1.2 convert_element_type.48
  64.1 1.5 dynamic_update_slice.48
  65.6 1.4 dynamic_update_slice.49
  67.1 1.5 dynamic_update_slice.50
  68.6 1.5 dynamic_update_slice.51
  70.0 1.5 dynamic_update_slice.52
  72.2 1.5 dynamic_update_slice.53
  73.7 1.5 dynamic_update_slice.54
  75.2 1.5 dynamic_update_slice.55
  76.7 1.5 dynamic_update_slice.56
  78.2 1.5 dynamic_update_slice.57
  79.7 1.5 dynamic_update_slice.58
  81.2 1.5 dynamic_update_slice.59
  82.8 1.5 dynamic_update_slice.60
  84.3 1.5 dynamic_update_slice.61
  85.8 1.5 dynamic_update_slice.62
  87.4 1.5 dynamic_update_slice.63
  88.9 3.8 %gather_fusion = bf16[192,1536]{1,0:T(8,128)(2,1)} fusion(bf16[192,1536]{1,0:T(8,128)(2,1)} %dynamic_update_slice.63, s32[1024]{0:T(1024)} %pad_clamp_fusion), kind=kCustom, calls=%fused_computation | custom fusion | bytes 1180416 | tf_op jit(solution)/shard_map/jit(_take)/gather | solution.py:102
  92.7 1.5 convolution_convert_fusion.1
  94.8 1.9 collective-permute-start.15
  96.7 1.3 collective-permute-start.16
  97.9 1.5 slice_reduce_fusion.2
  99.4 2.1 reshape.38
  101.5 1.9 maximum_convert_fusion
  103.4 7.5 %multiply_reduce_fusion.3 = (f32[1536]{0:T(1024)S(1)}, f32[1536]{0:T(1024)S(1)}, f32[1536]{0:T(1024)S(1)}, f32[128]{0:T(128)S(1)}, bf16[128,1536]{1,0:T(8,128)(2,1)}, /*index=5*/f32[128,1536]{1,0:T(8,128)S(1)}) fusion(f32[144,1536]{1,0:T(8,128)} %maximum_convert_fusion, f32[1536]{0:T(1024)S(1)} %get-tuple-element.76, f32[1536]{0:T(1024)} %get-tuple-element.77, ...), kind=kOutput, calls=%fused_computation.34 | convolution fusion | flops 1114172800 | bytes 12947968 | tf_op jit(solution)/shard_map/dot_general | solution.py:136
  113.0 2.5 convolution_convert_fusion.2
  116.6 64.1 %psum.7 = f32[3,1536]{1,0:T(4,128)S(1)} all-reduce(f32[3,1536]{1,0:T(4,128)S(1)} %pad_maximum_fusion), channel_id=1, replica_groups=mesh['groups'=2,'seq'=16] {'seq'}, use_global_device_ids=true, to_apply=%region_8.9 | all-reduce | flops 4608 | bytes 36864 | tf_op jit(solution)/shard_map/psum | solution.py:116
  181.3 2.6 copy.18
  183.8 88.8 %while.15 = (s32[]{:T(128)}, f32[1024]{0:T(1024)S(1)}, f32[1024]{0:T(1024)S(1)}, f32[1024,192]{0,1:T(8,128)}, bf16[16,128,320]{2,1,0:T(8,128)(2,1)}, /*index=5*/bf16[1024,128]{1,0:T(8,128)(2,1)S(1)}, s32[]{:T(128)}, s32[]{:T(128)}) while((s32[]{:T(128)}, f32[1024]{0:T(1024)S(1)}, f32[1024]{0:T(1024)S(1)}, f32[1024,192]{0,1:T(8,128)}, ...), condition=%wide.region_4.5_spmd.clone, body=%wide.region_1.4_spmd.clone.sunk | while | flops 85267456 | bytes 3735653 | solution.py:72
  185.8 1.1 fusion.41
  186.9 2.2 convolution_add_fusion.3
  192.2 2.5 convolution_add_fusion.3
  197.8 2.5 convolution_add_fusion.3
  203.4 2.5 convolution_add_fusion.3
  208.9 2.5 convolution_add_fusion.3
  214.5 2.5 convolution_add_fusion.3
  220.1 2.5 convolution_add_fusion.3
  225.6 2.5 convolution_add_fusion.3
  231.2 2.5 convolution_add_fusion.3
  236.8 2.5 convolution_add_fusion.3
  242.3 2.5 convolution_add_fusion.3
  247.9 2.5 convolution_add_fusion.3
  253.5 2.5 convolution_add_fusion.3
  259.0 2.5 convolution_add_fusion.3
  264.6 2.5 convolution_add_fusion.3
  270.2 2.5 convolution_add_fusion.3
  272.6 1.2 divide_convert_fusion
  274.9 1.5 convert_element_type.46
  276.4 4.1 %fusion.8 = bf16[128,1536]{1,0:T(8,128)(2,1)} fusion(f32[128,1536]{1,0:T(8,128)} %copy-done.1, bf16[128,1536]{1,0:T(8,128)(2,1)S(1)} %convert_element_type.46, bf16[1536,1536]{1,0:T(8,128)(2,1)} %param.18), kind=kOutput, calls=%fused_computation.19 | convolution fusion | flops 604372992 | bytes 6291456 | tf_op jit(solution)/shard_map/dot_general | solution.py:77
  (157 shorter events, 59.7 us)
Async XLA Ops:
  7.2 105.9 %copy-start = (bf16[1536,1024]{1,0:T(8,128)(2,1)S(1)}, bf16[1536,1024]{1,0:T(8,128)(2,1)}, u32[]{:S(2)}) copy-start(bf16[1536,1024]{1,0:T(8,128)(2,1)} %param.16) | copy-start | bytes 9437188
  7.2 96.2 %all-gather.3.cloned.1.call-start = ((), (), s32[]{:S(2)}) async-start(), calls=%async_computation.1 | async-start | bytes 9191424 | tf_op jit(solution)/shard_map/all_gather | solution.py:138
  7.9 7.6 %collective-permute-start = (bf16[12,1536]{1,0:T(8,128)(2,1)}, bf16[12,1536]{1,0:T(8,128)(2,1)S(1)}, u32[]{:S(2)}, u32[]{:S(2)}) collective-permute-start(bf16[12,1536]{1,0:T(8,128)(2,1)} %param.20), channel_id=1, source_target_pairs={{0,1},{1,2},{2,3},{3,4},{4,5},{5,6},{6,7},{7,8},{8,9},{9,10},{10,1... | collective-permute-start | bytes 110600 | tf_op jit(solution)/shard_map/ppermute | solution.py:93
  8.4 7.1 %collective-permute-start.1 = (bf16[12,1536]{1,0:T(8,128)(2,1)}, bf16[12,1536]{1,0:T(8,128)(2,1)S(1)}, u32[]{:S(2)}, u32[]{:S(2)}) collective-permute-start(bf16[12,1536]{1,0:T(8,128)(2,1)} %param.20), channel_id=1, source_target_pairs={{0,15},{1,0},{2,1},{3,2},{4,3},{5,4},{6,5},{7,6},{8,7},{9,8},{10,9... | collective-permute-start | bytes 110600 | tf_op jit(solution)/shard_map/ppermute | solution.py:98
  15.5 6.2 %collective-permute-start.2 = (bf16[12,1536]{1,0:T(8,128)(2,1)S(1)}, bf16[12,1536]{1,0:T(8,128)(2,1)S(1)}, u32[]{:S(2)}, u32[]{:S(2)}) collective-permute-start(bf16[12,1536]{1,0:T(8,128)(2,1)S(1)} %collective-permute-done), channel_id=1, source_target_pairs={{0,1},{1,2},{2,3},{3,4},{4,5},{5,6},{6,7},{7,8},{8,9},{9,10},{10,1... | collective-permute-start | bytes 110600 | tf_op jit(solution)/shard_map/ppermute | solution.py:93
  15.5 6.2 %collective-permute-start.3 = (bf16[12,1536]{1,0:T(8,128)(2,1)S(1)}, bf16[12,1536]{1,0:T(8,128)(2,1)S(1)}, u32[]{:S(2)}, u32[]{:S(2)}) collective-permute-start(bf16[12,1536]{1,0:T(8,128)(2,1)S(1)} %collective-permute-done.1), channel_id=1, source_target_pairs={{0,15},{1,0},{2,1},{3,2},{4,3},{5,4},{6,5},{7,6},{8,7},{9,8},{10,9... | collective-permute-start | bytes 110600 | tf_op jit(solution)/shard_map/ppermute | solution.py:98
  21.7 7.0 %collective-permute-start.4 = (bf16[12,1536]{1,0:T(8,128)(2,1)S(1)}, bf16[12,1536]{1,0:T(8,128)(2,1)S(1)}, u32[]{:S(2)}, u32[]{:S(2)}) collective-permute-start(bf16[12,1536]{1,0:T(8,128)(2,1)S(1)} %collective-permute-done.2), channel_id=1, source_target_pairs={{0,1},{1,2},{2,3},{3,4},{4,5},{5,6},{6,7},{7,8},{8,9},{9,10},{10,1... | collective-permute-start | bytes 110600 | tf_op jit(solution)/shard_map/ppermute | solution.py:93
  21.7 7.9 %collective-permute-start.5 = (bf16[12,1536]{1,0:T(8,128)(2,1)S(1)}, bf16[12,1536]{1,0:T(8,128)(2,1)S(1)}, u32[]{:S(2)}, u32[]{:S(2)}) collective-permute-start(bf16[12,1536]{1,0:T(8,128)(2,1)S(1)} %collective-permute-done.3), channel_id=1, source_target_pairs={{0,15},{1,0},{2,1},{3,2},{4,3},{5,4},{6,5},{7,6},{8,7},{9,8},{10,9... | collective-permute-start | bytes 110600 | tf_op jit(solution)/shard_map/ppermute | solution.py:98
  28.7 7.2 %collective-permute-start.6 = (bf16[12,1536]{1,0:T(8,128)(2,1)S(1)}, bf16[12,1536]{1,0:T(8,128)(2,1)S(1)}, u32[]{:S(2)}, u32[]{:S(2)}) collective-permute-start(bf16[12,1536]{1,0:T(8,128)(2,1)S(1)} %collective-permute-done.4), channel_id=1, source_target_pairs={{0,1},{1,2},{2,3},{3,4},{4,5},{5,6},{6,7},{7,8},{8,9},{9,10},{10,1... | collective-permute-start | bytes 110600 | tf_op jit(solution)/shard_map/ppermute | solution.py:93
  29.6 12.9 %collective-permute-start.7 = (bf16[12,1536]{1,0:T(8,128)(2,1)S(1)}, bf16[12,1536]{1,0:T(8,128)(2,1)}, u32[]{:S(2)}, u32[]{:S(2)}) collective-permute-start(bf16[12,1536]{1,0:T(8,128)(2,1)S(1)} %collective-permute-done.5), channel_id=1, source_target_pairs={{0,15},{1,0},{2,1},{3,2},{4,3},{5,4},{6,5},{7,6},{8,7},{9,8},{10,9... | collective-permute-start | bytes 110600 | tf_op jit(solution)/shard_map/ppermute | solution.py:98
  35.9 11.0 %collective-permute-start.8 = (bf16[12,1536]{1,0:T(8,128)(2,1)S(1)}, bf16[12,1536]{1,0:T(8,128)(2,1)}, u32[]{:S(2)}, u32[]{:S(2)}) collective-permute-start(bf16[12,1536]{1,0:T(8,128)(2,1)S(1)} %collective-permute-done.6), channel_id=1, source_target_pairs={{0,1},{1,2},{2,3},{3,4},{4,5},{5,6},{6,7},{7,8},{8,9},{9,10},{10,1... | collective-permute-start | bytes 110600 | tf_op jit(solution)/shard_map/ppermute | solution.py:93
  36.6 34.9 %all-to-all-start = ((bf16[16,128,12]{1,2,0:T(8,128)(2,1)}), bf16[16,128,12]{1,2,0:T(8,128)(2,1)S(1)}, u32[]{:S(2)}, u32[]{:S(2)}) async-start(bf16[16,128,12]{1,2,0:T(8,128)(2,1)} %copy.17), calls=%async_computation | async-start | bytes 131072 | tf_op jit(solution)/shard_map/all_to_all | solution.py:84
  42.4 138.8 %all-gather.5.cloned.1.call-start = ((), (), s32[]{:S(2)}) async-start(), calls=%async_computation.2 | async-start | bytes 1392640 | tf_op jit(solution)/shard_map/all_gather | solution.py:66
  42.5 6.5 %collective-permute-start.9 = (bf16[12,1536]{1,0:T(8,128)(2,1)}, bf16[12,1536]{1,0:T(8,128)(2,1)S(1)}, u32[]{:S(2)}, u32[]{:S(2)}) collective-permute-start(bf16[12,1536]{1,0:T(8,128)(2,1)} %collective-permute-done.7), channel_id=1, source_target_pairs={{0,15},{1,0},{2,1},{3,2},{4,3},{5,4},{6,5},{7,6},{8,7},{9,8},{10,9... | collective-permute-start | bytes 110600 | tf_op jit(solution)/shard_map/ppermute | solution.py:98
  46.9 7.1 %collective-permute-start.10 = (bf16[12,1536]{1,0:T(8,128)(2,1)}, bf16[12,1536]{1,0:T(8,128)(2,1)S(1)}, u32[]{:S(2)}, u32[]{:S(2)}) collective-permute-start(bf16[12,1536]{1,0:T(8,128)(2,1)} %collective-permute-done.8), channel_id=1, source_target_pairs={{0,1},{1,2},{2,3},{3,4},{4,5},{5,6},{6,7},{7,8},{8,9},{9,10},{10,1... | collective-permute-start | bytes 110600 | tf_op jit(solution)/shard_map/ppermute | solution.py:93
  49.0 0.6 copy-start.3
  49.6 7.1 %collective-permute-start.11 = (bf16[12,1536]{1,0:T(8,128)(2,1)S(1)}, bf16[12,1536]{1,0:T(8,128)(2,1)}, u32[]{:S(2)}, u32[]{:S(2)}) collective-permute-start(bf16[12,1536]{1,0:T(8,128)(2,1)S(1)} %collective-permute-done.9), channel_id=1, source_target_pairs={{0,15},{1,0},{2,1},{3,2},{4,3},{5,4},{6,5},{7,6},{8,7},{9,8},{10,9... | collective-permute-start | bytes 110600 | tf_op jit(solution)/shard_map/ppermute | solution.py:98
  54.1 2.7 copy-start.4
  54.1 7.4 %collective-permute-start.12 = (bf16[12,1536]{1,0:T(8,128)(2,1)S(1)}, bf16[12,1536]{1,0:T(8,128)(2,1)}, u32[]{:S(2)}, u32[]{:S(2)}) collective-permute-start(bf16[12,1536]{1,0:T(8,128)(2,1)S(1)} %collective-permute-done.10), channel_id=1, source_target_pairs={{0,1},{1,2},{2,3},{3,4},{4,5},{5,6},{6,7},{7,8},{8,9},{9,10},{10,1... | collective-permute-start | bytes 110600 | tf_op jit(solution)/shard_map/ppermute | solution.py:93
  56.7 29.1 %collective-permute-start.13 = (bf16[12,1536]{1,0:T(8,128)(2,1)}, bf16[12,1536]{1,0:T(8,128)(2,1)}, u32[]{:S(2)}, u32[]{:S(2)}) collective-permute-start(bf16[12,1536]{1,0:T(8,128)(2,1)} %collective-permute-done.11), channel_id=1, source_target_pairs={{0,15},{1,0},{2,1},{3,2},{4,3},{5,4},{6,5},{7,6},{8,7},{9,8},{10,9... | collective-permute-start | bytes 110600 | tf_op jit(solution)/shard_map/ppermute | solution.py:98
  61.5 25.9 %collective-permute-start.14 = (bf16[12,1536]{1,0:T(8,128)(2,1)}, bf16[12,1536]{1,0:T(8,128)(2,1)}, u32[]{:S(2)}, u32[]{:S(2)}) collective-permute-start(bf16[12,1536]{1,0:T(8,128)(2,1)} %collective-permute-done.12), channel_id=1, source_target_pairs={{0,1},{1,2},{2,3},{3,4},{4,5},{5,6},{6,7},{7,8},{8,9},{9,10},{10,1... | collective-permute-start | bytes 110600 | tf_op jit(solution)/shard_map/ppermute | solution.py:93
  76.7 16.0 %copy-start.6 = (pred[192]{0:T(512)(128)(4,1)S(1)}, pred[192]{0:T(512)(128)(4,1)}, u32[]{:S(2)}) copy-start(pred[192]{0:T(512)(128)(4,1)} %compare_and_fusion) | copy-start | bytes 580
  76.7 16.0 %copy-start.7 = (bf16[192]{0:T(256)(128)(2,1)S(1)}, bf16[192]{0:T(256)(128)(2,1)}, u32[]{:S(2)}) copy-start(bf16[192]{0:T(256)(128)(2,1)} %convert_element_type.48) | copy-start | bytes 1156
  94.8 6.8 %collective-permute-start.15 = (bf16[8,1536]{1,0:T(8,128)(2,1)}, bf16[8,1536]{1,0:T(8,128)(2,1)}, u32[]{:S(2)}, u32[]{:S(2)}) collective-permute-start(bf16[8,1536]{1,0:T(8,128)(2,1)} %get-tuple-element.95), channel_id=1, source_target_pairs={{0,1},{1,2},{2,3},{3,4},{4,5},{5,6},{6,7},{7,8},{8,9},{9,10},{10,1... | collective-permute-start | bytes 73736 | tf_op jit(solution)/shard_map/ppermute | solution.py:21
  96.7 4.9 %collective-permute-start.16 = (bf16[8,1536]{1,0:T(8,128)(2,1)}, bf16[8,1536]{1,0:T(8,128)(2,1)}, u32[]{:S(2)}, u32[]{:S(2)}) collective-permute-start(bf16[8,1536]{1,0:T(8,128)(2,1)} %get-tuple-element.96), channel_id=1, source_target_pairs={{1,0},{2,1},{3,2},{4,3},{5,4},{6,5},{7,6},{8,7},{9,8},{10,9},{11,1... | collective-permute-start | bytes 73736 | tf_op jit(solution)/shard_map/ppermute | solution.py:23
  103.4 8.4 %copy-start.2 = (bf16[1536,320]{0,1:T(8,128)(2,1)S(1)}, bf16[1536,320]{0,1:T(8,128)(2,1)}, u32[]{:S(2)}) copy-start(bf16[1536,320]{0,1:T(8,128)(2,1)} %param.17) | copy-start | bytes 2949124
  103.4 8.4 %copy-start.5 = (f32[1536]{0:T(1024)S(1)}, f32[1536]{0:T(1024)}, u32[]{:S(2)}) copy-start(f32[1536]{0:T(1024)} %param.15) | copy-start | bytes 18436
  110.9 0.9 copy-start.1
Sparse Core Ops, SparseCore 0:
  10.3 83.1 all-gather.2
  113.1 41.4 all-gather.4
